TPU v7x, 32 devices: a whole 2x2x4 slice. The times are simulated.
32 devices in a mesh: fsdp: 4 (over y, core), tensor: 8 (over z, x).
Axes of the slice: x: 2, y: 2, z: 4, core: 2. Of those that a mesh axis runs over, the one named last changes fastest.
Arguments:
- activations: bfloat16 [4096, 8192], P('fsdp', 'tensor'), may hold values from -6 to 6
- first_factor: bfloat16 [64, 128, 512], P('tensor', 'fsdp'), may hold values from -0.5 to 0.5
- second_factor: bfloat16 [64, 512, 512], P('tensor', 'fsdp'), may hold values from -0.25 to 0.25
- third_factor: bfloat16 [64, 512, 512], P('tensor', 'fsdp'), may hold values from -0.25 to 0.25
- fourth_factor: bfloat16 [64, 512, 128], P('tensor', 'fsdp'), may hold values from -0.25 to 0.25
- out_grad: bfloat16 [4096, 8192], P('fsdp', 'tensor'), may hold values from -6 to 6
Outputs:
- result: bfloat16 [4096, 8192], P('fsdp', 'tensor')
- in_grad: bfloat16 [4096, 8192], P('fsdp', 'tensor')
- first_grad: float32 [64, 128, 512], P('tensor', 'fsdp')
- second_grad: float32 [64, 512, 512], P('tensor', 'fsdp')
- third_grad: float32 [64, 512, 512], P('tensor', 'fsdp')
- fourth_grad: float32 [64, 512, 128], P('tensor', 'fsdp')
All inputs are finite; a program needn't handle non-finite values.
Results may differ from a plain program's by a relative error of at most 0.014.
Values may be sent and summed in bfloat16 or wider, within the bound.
A program may use at most 128 MiB of HBM per device.

v0:
```python
import jax
import jax.numpy as jnp
from jax import lax
from jax.sharding import PartitionSpec as P

D = 8192
NB = 64
HB = 512


def gelu_value(v):
    return 0.5 * v * (1.0 + lax.erf(v * 0.7071067811865476))


def gelu_slope(v):
    return (
        0.5 * (1.0 + lax.erf(v * 0.7071067811865476))
        + v * jnp.exp(-0.5 * v * v) * 0.3989422804014327
    )


def fetch_first(shard):
    return lax.all_gather(shard, "fsdp", axis=1, tiled=True)


def fetch_second(shard):
    return lax.all_gather(shard, "fsdp", axis=1, tiled=True)


def fetch_third(shard):
    return lax.all_gather(shard, "fsdp", axis=1, tiled=True)


def fetch_fourth(shard):
    return lax.all_gather(shard, "fsdp", axis=1, tiled=True)


def split_units(arr):
    return arr.reshape(arr.shape[0], NB, HB // NB, arr.shape[2])


def join_units(received):
    local_blocks = received.shape[1]
    return received.transpose(1, 0, 2, 3).reshape(local_blocks, HB, received.shape[3])


def local(activations, first_factor, second_factor, third_factor, fourth_factor, out_grad):
    f32 = jnp.float32
    bf16 = jnp.bfloat16
    tok = activations.shape[0]
    local_blocks = second_factor.shape[0]
    block_in = D // NB
    inputs = activations.reshape(tok, local_blocks, block_in)
    factors = (
        fetch_first(first_factor),
        fetch_second(second_factor),
        fetch_third(third_factor),
        fetch_fourth(fourth_factor),
    )
    wone, wtwo, wthree, wfour = factors
    first_out = jnp.einsum("tbi,bij->bjt", inputs, wone, preferred_element_type=f32).astype(bf16)
    mixed_part = join_units(
        lax.all_to_all(split_units(first_out), "tensor", split_axis=1, concat_axis=0, tiled=True)
    )
    pre_part = jnp.einsum("cpt,cpm->cmt", mixed_part, wtwo, preferred_element_type=f32)
    hidden_part = gelu_value(pre_part).astype(bf16)
    down_part = jnp.einsum("cmt,cmn->cnt", hidden_part, wthree, preferred_element_type=f32).astype(
        bf16
    )
    back = lax.all_to_all(split_units(down_part), "tensor", split_axis=1, concat_axis=0, tiled=True)
    regrouped = join_units(back)
    result = jnp.einsum("bpt,bpo->tbo", regrouped, wfour, preferred_element_type=f32).astype(bf16)
    result = result.reshape(tok, local_blocks * block_in)
    vone, vtwo, vthree, vfour = (
        fetch_first(first_factor),
        fetch_second(second_factor),
        fetch_third(third_factor),
        fetch_fourth(fourth_factor),
    )
    grad_out = out_grad.reshape(tok, local_blocks, block_in)
    fourth_grad = jnp.einsum("bpt,tbo->bpo", regrouped, grad_out, preferred_element_type=f32)
    dw = jnp.einsum("tbo,bpo->bpt", grad_out, vfour, preferred_element_type=f32).astype(bf16)
    ddown = join_units(
        lax.all_to_all(split_units(dw), "tensor", split_axis=1, concat_axis=0, tiled=True)
    )
    again_out = jnp.einsum("tbi,bij->bjt", inputs, vone, preferred_element_type=f32).astype(bf16)
    mixed_in = join_units(
        lax.all_to_all(split_units(again_out), "tensor", split_axis=1, concat_axis=0, tiled=True)
    )
    pre = jnp.einsum("cpt,cpm->cmt", mixed_in, vtwo, preferred_element_type=f32)
    hidden = gelu_value(pre).astype(bf16)
    third_grad = jnp.einsum("cmt,cnt->cmn", hidden, ddown, preferred_element_type=f32)
    dhidden = jnp.einsum("cnt,cmn->cmt", ddown, vthree, preferred_element_type=f32)
    dpre = (dhidden * gelu_slope(pre)).astype(bf16)
    second_grad = jnp.einsum("cpt,cmt->cpm", mixed_in, dpre, preferred_element_type=f32)
    dz = jnp.einsum("cmt,cpm->cpt", dpre, vtwo, preferred_element_type=f32).astype(bf16)
    dy = join_units(
        lax.all_to_all(split_units(dz), "tensor", split_axis=1, concat_axis=0, tiled=True)
    )
    first_grad = jnp.einsum("tbi,bjt->bij", inputs, dy, preferred_element_type=f32)
    in_grad = jnp.einsum("bjt,bij->tbi", dy, vone, preferred_element_type=f32).astype(bf16)
    in_grad = in_grad.reshape(tok, local_blocks * block_in)
    shares = (
        lax.psum_scatter(
            first_grad.astype(jnp.bfloat16), "fsdp", scatter_dimension=1, tiled=True
        ).astype(jnp.float32),
        lax.psum_scatter(
            second_grad.astype(jnp.bfloat16), "fsdp", scatter_dimension=1, tiled=True
        ).astype(jnp.float32),
        lax.psum_scatter(
            third_grad.astype(jnp.bfloat16), "fsdp", scatter_dimension=1, tiled=True
        ).astype(jnp.float32),
        lax.psum_scatter(
            fourth_grad.astype(jnp.bfloat16), "fsdp", scatter_dimension=1, tiled=True
        ).astype(jnp.float32),
    )
    return (result, in_grad, shares[0], shares[1], shares[2], shares[3])


def solution(mesh):
    in_specs = (
        P("fsdp", "tensor"),
        P("tensor", "fsdp", None),
        P("tensor", "fsdp", None),
        P("tensor", "fsdp", None),
        P("tensor", "fsdp", None),
        P("fsdp", "tensor"),
    )
    out_specs = (
        P("fsdp", "tensor"),
        P("fsdp", "tensor"),
        P("tensor", "fsdp", None),
        P("tensor", "fsdp", None),
        P("tensor", "fsdp", None),
        P("tensor", "fsdp", None),
    )
    return jax.shard_map(local, mesh=mesh, in_specs=in_specs, out_specs=out_specs, check_vma=False)
```

profile of v0, /device:TPU:0, one launch (start us, length us, event | category | flops | bytes accessed | tf_op | source)
XLA Modules:
  0.0 903.7 jit_solution(2316316129718884985)
XLA Ops:
  7.2 0.0 copy-start
  7.2 0.0 all-gather.11.cloned.1.call-start
  7.2 1.9 copy.62
  9.2 0.0 all-gather.11.cloned.1.call-update
  9.2 20.5 %all-gather.11.cloned.1.call-done = bf16[8,512,128]{1,2,0:T(8,128)(2,1)} async-done(((bf16[8,128,128]{1,2,0:T(8,128)(2,1)}), bf16[8,512,128]{1,2,0:T(8,128)(2,1)}) %all-gather.11.cloned.1.call-update) | async-done | bytes 1048592 | tf_op jit(solution)/shard_map/all_gather | solution.py:35
  29.7 7.6 convert_bitcast_fusion.1
  37.3 8.1 copy.65
  45.4 5.5 all-to-all-start.2
  50.9 0.0 all-gather.5.cloned.1.call-start
  50.9 0.7 all-gather.5.cloned.1.call-update
  51.7 18.9 %all-gather.5.cloned.1.call-done = bf16[8,128,512]{2,1,0:T(8,128)(2,1)} async-done(((bf16[8,32,512]{2,1,0:T(8,128)(2,1)}), bf16[8,128,512]{2,1,0:T(8,128)(2,1)}) %all-gather.5.cloned.1.call-update) | async-done | bytes 1048592 | tf_op jit(solution)/shard_map/all_gather | solution.py:23
  70.5 0.0 copy-done
  70.5 6.8 convert_bitcast_fusion.3
  77.4 8.0 copy.55
  85.4 149.0 %all-to-all-done.2 = bf16[8,64,8,1024]{3,2,0,1:T(8,128)(2,1)} async-done(((bf16[8,64,8,1024]{3,2,0,1:T(8,128)(2,1)}), bf16[8,64,8,1024]{3,2,0,1:T(8,128)(2,1)}, u32[]{:S(2)}, u32[]{:S(2)}) %all-to-all-start.2) | async-done | bytes 8388640 | tf_op jit(solution)/shard_map/all_to_all | solution.py:84
  234.5 5.0 all-to-all-start
  239.5 0.0 all-gather.7.cloned.1.call-start
  239.5 0.7 all-gather.7.cloned.1.call-update
  240.2 0.5 all-gather.9.cloned.1.call-start
  240.7 0.0 copy-done.3
  240.7 1.3 copy.58
  242.0 0.0 all-gather.9.cloned.1.call-update
  242.1 9.0 %copy.66 = bf16[8,8,8,8,1024]{4,3,0,1,2:T(8,128)(2,1)} copy(bf16[8,8,8,8,1024]{4,3,0,2,1:T(8,128)(2,1)} %bitcast.17) | data formatting | bytes 16777216 | tf_op jit(solution)/shard_map/all_to_all | solution.py:84
  251.1 171.0 %all-to-all-done = bf16[8,64,8,1024]{3,2,0,1:T(8,128)(2,1)} async-done(((bf16[8,64,8,1024]{3,2,0,1:T(8,128)(2,1)}), bf16[8,64,8,1024]{3,2,0,1:T(8,128)(2,1)}, u32[]{:S(2)}, u32[]{:S(2)}) %all-to-all-start) | async-done | bytes 8388640 | tf_op jit(solution)/shard_map/all_to_all | solution.py:63
  422.1 8.5 copy.56
  430.6 14.5 %fusion.7 = (bf16[8,512,1024]{1,2,0:T(8,128)(2,1)}, f32[8,1024,512]{2,1,0:T(8,128)}) fusion(bf16[8,512,1024]{2,1,0:T(8,128)(2,1)} %bitcast.126, bf16[8,512,512]{2,1,0:T(8,128)(2,1)} %all-gather.7.cloned.1.call-done), kind=kOutput, calls=%fused_computation.10 | convolution fusion | flops 4315938816 | bytes 37748736 | tf_op jit(solution)/shard_map/cpt,cpm->cmt/dot_general | solution.py:65
  445.1 14.2 %fusion.5 = bf16[8,512,1024]{1,2,0:T(8,128)(2,1)S(1)} fusion(f32[8,1024,512]{2,1,0:T(8,128)} %get-tuple-element.25, bf16[8,512,1024]{2,1,0:T(8,128)(2,1)} %bitcast.128, bf16[8,512,512]{1,2,0:T(8,128)(2,1)} %all-gather.9.cloned.1.call-done), kind=kOutput, calls=%fused_computation.6 | convolution fusion | flops 4336910336 | bytes 37748736 | tf_op jit(solution)/shard_map/cnt,cmn->cmt/dot_general | solution.py:93
  459.3 0.0 copy-start.5
  459.3 3.3 copy-done.5
  462.6 0.0 copy-done.4
  462.6 6.7 convert_bitcast_fusion
  469.3 8.0 copy.70
  477.3 5.0 all-to-all-start.3
  482.4 0.2 reduce-scatter.9.cloned.1.call-start
  482.6 11.0 %convolution_convert_fusion = bf16[8,512,512]{2,1,0:T(8,128)(2,1)} fusion(bf16[8,512,1024]{1,2,0:T(8,128)(2,1)} %get-tuple-element.24, bf16[8,512,1024]{2,1,0:T(8,128)(2,1)} %bitcast.129), kind=kOutput, calls=%fused_computation.17 | convolution fusion | flops 4297064448 | bytes 20971520 | tf_op jit(solution)/shard_map/cmt,cnt->cmn/dot_general | solution.py:92
  493.6 0.0 reduce-scatter.9.cloned.1.call-update
  493.7 10.4 %convert_bitcast_fusion.2 = bf16[8,64,8,1024]{3,2,1,0:T(8,128)(2,1)} fusion(bf16[8,512,1024]{1,2,0:T(8,128)(2,1)} %get-tuple-element.24, bf16[8,512,512]{1,2,0:T(8,128)(2,1)} %all-gather.9.cloned.1.call-done), kind=kOutput, calls=%fused_computation.15 | convolution fusion | flops 4299161600 | bytes 20971520 | tf_op jit(solution)/shard_map/cmt,cmn->cnt/dot_general | solution.py:67
  504.1 8.3 copy.60
  512.3 152.0 %all-to-all-done.3 = bf16[8,64,8,1024]{3,2,0,1:T(8,128)(2,1)} async-done(((bf16[8,64,8,1024]{3,2,0,1:T(8,128)(2,1)}), bf16[8,64,8,1024]{3,2,0,1:T(8,128)(2,1)}, u32[]{:S(2)}, u32[]{:S(2)}) %all-to-all-start.3) | async-done | bytes 8388640 | tf_op jit(solution)/shard_map/all_to_all | solution.py:98
  664.3 5.0 all-to-all-start.1
  669.3 0.0 reduce-scatter.7.cloned.1.call-start
  669.3 12.2 %convolution_convert_fusion.1 = bf16[8,512,512]{2,1,0:T(8,128)(2,1)} fusion(bf16[8,512,1024]{2,1,0:T(8,128)(2,1)} %bitcast.127, bf16[8,512,1024]{1,2,0:T(8,128)(2,1)} %copy-done.5), kind=kOutput, calls=%fused_computation.18 | convolution fusion | flops 4297064448 | bytes 20971520 | tf_op jit(solution)/shard_map/cpt,cmt->cpm/dot_general | solution.py:95
  681.6 0.0 reduce-scatter.7.cloned.1.call-update
  681.6 0.3 reduce-scatter.5.cloned.1.call-start
  681.8 9.1 %copy.71 = bf16[8,8,8,8,1024]{4,3,1,0,2:T(8,128)(2,1)} copy(bf16[8,8,8,8,1024]{4,3,1,2,0:T(8,128)(2,1)} %bitcast.26) | data formatting | bytes 16777216 | tf_op jit(solution)/shard_map/all_to_all | solution.py:98
  691.0 6.1 fusion.26
  697.1 1.7 copy.73
  698.9 0.0 reduce-scatter.5.cloned.1.call-update
  698.9 0.0 reduce-scatter.11.cloned.1.call-start
  698.9 152.5 %all-to-all-done.1 = bf16[8,64,8,1024]{3,2,0,1:T(8,128)(2,1)} async-done(((bf16[8,64,8,1024]{3,2,0,1:T(8,128)(2,1)}), bf16[8,64,8,1024]{3,2,0,1:T(8,128)(2,1)}, u32[]{:S(2)}, u32[]{:S(2)}) %all-to-all-start.1) | async-done | bytes 8388640 | tf_op jit(solution)/shard_map/all_to_all | solution.py:70
  851.5 8.5 copy.61
  860.0 0.0 copy-done.2
  860.0 6.8 fusion.23
  866.8 0.0 reduce-scatter.11.cloned.1.call-update
  866.8 0.0 reduce-scatter.9.cloned.1.call-done
  866.9 2.8 convert_element_type.83
  869.7 3.0 convert_element_type.81
  872.6 6.5 convolution_convert_fusion.2
  879.1 4.0 copy.78
  883.1 0.0 copy-done.1
  883.1 6.0 convolution_convert_fusion.3
  889.1 3.9 copy.77
  893.0 1.8 copy.79
  894.8 1.8 convert_element_type.85
  (9 shorter events, 0.0 us)
Async XLA Ops:
  7.2 63.4 %copy-start = (bf16[1024,1024]{1,0:T(8,128)(2,1)S(1)}, bf16[1024,1024]{1,0:T(8,128)(2,1)}, u32[]{:S(2)}) copy-start(bf16[1024,1024]{1,0:T(8,128)(2,1)} %param.6) | copy-start | bytes 6291460
  7.2 22.5 %all-gather.11.cloned.1.call-start = ((), (), s32[]{:S(2)}) async-start(), calls=%async_computation.11 | async-start | bytes 1310720 | tf_op jit(solution)/shard_map/all_gather | solution.py:35
  45.4 189.1 %all-to-all-start.2 = ((bf16[8,64,8,1024]{3,2,0,1:T(8,128)(2,1)}), bf16[8,64,8,1024]{3,2,0,1:T(8,128)(2,1)}, u32[]{:S(2)}, u32[]{:S(2)}) async-start(bf16[8,64,8,1024]{3,2,0,1:T(8,128)(2,1)} %copy.65), calls=%async_computation.2 | async-start | bytes 16777216 | tf_op jit(solution)/shard_map/all_to_all | solution.py:84
  50.9 19.6 %all-gather.5.cloned.1.call-start = ((), (), s32[]{:S(2)}) async-start(), calls=%async_computation.8 | async-start | bytes 1310720 | tf_op jit(solution)/shard_map/all_gather | solution.py:23
  85.4 155.3 %copy-start.3 = (bf16[8,128,512]{2,1,0:T(8,128)(2,1)S(1)}, bf16[8,128,512]{2,1,0:T(8,128)(2,1)}, u32[]{:S(2)}) copy-start(bf16[8,128,512]{2,1,0:T(8,128)(2,1)} %param.9) | copy-start | bytes 3145732
  234.5 187.6 %all-to-all-start = ((bf16[8,64,8,1024]{3,2,0,1:T(8,128)(2,1)}), bf16[8,64,8,1024]{3,2,0,1:T(8,128)(2,1)}, u32[]{:S(2)}, u32[]{:S(2)}) async-start(bf16[8,64,8,1024]{3,2,0,1:T(8,128)(2,1)} %copy.55), calls=%async_computation | async-start | bytes 16777216 | tf_op jit(solution)/shard_map/all_to_all | solution.py:63
  239.5 191.1 %all-gather.7.cloned.1.call-start = ((), (), s32[]{:S(2)}) async-start(), calls=%async_computation.9 | async-start | bytes 5242880 | tf_op jit(solution)/shard_map/all_gather | solution.py:27
  240.2 204.9 %all-gather.9.cloned.1.call-start = ((), (), s32[]{:S(2)}) async-start(), calls=%async_computation.10 | async-start | bytes 5242880 | tf_op jit(solution)/shard_map/all_gather | solution.py:31
  445.1 17.5 %copy-start.4 = (bf16[8,512,512]{2,1,0:T(8,128)(2,1)S(1)}, bf16[8,512,512]{2,1,0:T(8,128)(2,1)}, u32[]{:S(2)}) copy-start(bf16[8,512,512]{2,1,0:T(8,128)(2,1)} %all-gather.7.cloned.1.call-done) | copy-start | bytes 12582916
  459.3 3.3 copy-start.5
  477.3 187.0 %all-to-all-start.3 = ((bf16[8,64,8,1024]{3,2,0,1:T(8,128)(2,1)}), bf16[8,64,8,1024]{3,2,0,1:T(8,128)(2,1)}, u32[]{:S(2)}, u32[]{:S(2)}) async-start(bf16[8,64,8,1024]{3,2,0,1:T(8,128)(2,1)} %copy.70), calls=%async_computation.3 | async-start | bytes 16777216 | tf_op jit(solution)/shard_map/all_to_all | solution.py:98
  482.4 384.4 %reduce-scatter.9.cloned.1.call-start = ((), (), s32[]{:S(2)}) async-start(), calls=%async_computation.14 | async-start | bytes 5242880 | tf_op jit(solution)/shard_map/reduce_scatter | solution.py:110
  664.3 187.2 %all-to-all-start.1 = ((bf16[8,64,8,1024]{3,2,0,1:T(8,128)(2,1)}), bf16[8,64,8,1024]{3,2,0,1:T(8,128)(2,1)}, u32[]{:S(2)}, u32[]{:S(2)}) async-start(bf16[8,64,8,1024]{3,2,0,1:T(8,128)(2,1)} %copy.60), calls=%async_computation.1 | async-start | bytes 16777216 | tf_op jit(solution)/shard_map/all_to_all | solution.py:70
  669.3 200.4 %reduce-scatter.7.cloned.1.call-start = ((), (), s32[]{:S(2)}) async-start(), calls=%async_computation.13 | async-start | bytes 5242880 | tf_op jit(solution)/shard_map/reduce_scatter | solution.py:107
  681.6 211.4 %reduce-scatter.5.cloned.1.call-start = ((), (), s32[]{:S(2)}) async-start(), calls=%async_computation.12 | async-start | bytes 1310720 | tf_op jit(solution)/shard_map/reduce_scatter | solution.py:104
  698.9 196.0 %reduce-scatter.11.cloned.1.call-start = ((), (), s32[]{:S(2)}) async-start(), calls=%async_computation.15 | async-start | bytes 1310720 | tf_op jit(solution)/shard_map/reduce_scatter | solution.py:113
  851.5 8.6 copy-start.2
  872.6 10.4 %copy-start.1 = (bf16[8,512,128]{1,2,0:T(8,128)(2,1)S(1)}, bf16[8,512,128]{1,2,0:T(8,128)(2,1)}, u32[]{:S(2)}) copy-start(bf16[8,512,128]{1,2,0:T(8,128)(2,1)} %all-gather.11.cloned.1.call-done) | copy-start | bytes 3145732
Sparse Core Ops, SparseCore 0:
  10.1 19.5 all-gather.10
  53.3 17.1 all-gather.4
  241.9 34.8 all-gather.6
  278.7 35.0 all-gather.8
  493.8 44.8 reduce-scatter.8
  681.7 44.8 reduce-scatter.6
  729.1 24.8 reduce-scatter.4
  866.9 23.1 reduce-scatter.10
where the time goes:
time: 911 us; the launch traced here: 904 us
  waiting for transfers between devices  666 us (73%)
  matrix products  109 us (12%)
  local copies, waits for them, and re-layouts  85.6 us (9%)
  starting transfers between devices  21.7 us (2%)
  between operations  14.5 us (2%)
    all_to_all x1, waiting for transfers between devices, local(): lax.all_to_all(split_units(first_out), 'tensor', split_axis=1, concat_axi...  171 us
    all_to_all x1, waiting for transfers between devices, local(): lax.all_to_all(split_units(down_part), 'tensor', split_axis=1, concat_axi...  153 us
    all_to_all x1, waiting for transfers between devices, local(): lax.all_to_all(split_units(dz), 'tensor', split_axis=1, concat_axis=0, ti...  152 us
    all_to_all x1, waiting for transfers between devices, local(): lax.all_to_all(split_units(dw), 'tensor', split_axis=1, concat_axis=0, ti...  149 us
    reshape x4, local copies, waits for them, and re-layouts, split_units(): return arr.reshape(arr.shape[0], NB, HB // NB, arr.shape[2])  32.5 us
    all_gather x1, waiting for transfers between devices, fetch_fourth(): return lax.all_gather(shard, 'fsdp', axis=1, tiled=True)  20.5 us
    all_gather x1, waiting for transfers between devices, fetch_first(): return lax.all_gather(shard, 'fsdp', axis=1, tiled=True)  18.9 us
  transfers between devices with their start and end apart: 12, of which 6 were waited for; matrix products, arithmetic and copies ran while one was open for 17% of the time, Pallas kernels for 0%

commit v1 on v0

--- a/solution.py
+++ b/solution.py
@@ -95,7 +95,15 @@
     second_grad = jnp.einsum("cpt,cmt->cpm", mixed_in, dpre, preferred_element_type=f32)
     dz = jnp.einsum("cmt,cpm->cpt", dpre, vtwo, preferred_element_type=f32).astype(bf16)
     dy = join_units(
-        lax.all_to_all(split_units(dz), "tensor", split_axis=1, concat_axis=0, tiled=True)
+        jnp.concatenate(
+            lax.all_to_all(
+                jnp.stack(jnp.split(split_units(dz), lax.axis_size("tensor"), axis=1)),
+                "tensor",
+                0,
+                0,
+            ),
+            axis=0,
+        )
     )
     first_grad = jnp.einsum("tbi,bjt->bij", inputs, dy, preferred_element_type=f32)
     in_grad = jnp.einsum("bjt,bij->tbi", dy, vone, preferred_element_type=f32).astype(bf16)

time: 911 us -> 843 us (0.925)
  waiting for transfers between devices: 666 us -> 604 us
  local copies, waits for them, and re-layouts: 85.6 us -> 74.1 us
  matrix products: 109 us -> 120 us
    all_to_all x1, waiting for transfers between devices: 149 us -> 90 us  [local(): lax.all_to_all(split_units(dw), 'tensor', split_axis=1, concat_axis=0, ti...]
    all_to_all x1, waiting for transfers between devices: 153 us -> 122 us  [local(): lax.all_to_all(split_units(down_part), 'tensor', split_axis=1, concat_axi...]
    all_gather x1, waiting for transfers between devices: 0.01 us -> 26.1 us  [fetch_second(): return lax.all_gather(shard, 'fsdp', axis=1, tiled=True)]
    all_to_all x1, waiting for transfers between devices: 171 us -> 148 us  [local(): lax.all_to_all(split_units(first_out), 'tensor', split_axis=1, concat_axi...]
    all_gather x1, waiting for transfers between devices: 0.01 us -> 22.2 us  [fetch_third(): return lax.all_gather(shard, 'fsdp', axis=1, tiled=True)]
    all_to_all x1 -> x0, local copies, waits for them, and re-layouts: 9.15 us -> none  [local(): lax.all_to_all(split_units(dz), 'tensor', split_axis=1, concat_axis=0, ti...]
    reshape x4 -> x3, local copies, waits for them, and re-layouts: 32.5 us -> 24.2 us  [split_units(): return arr.reshape(arr.shape[0], NB, HB // NB, arr.shape[2])]
    unnamed x17 -> x22, local copies, waits for them, and re-layouts: 16.2 us -> 19.6 us
  transfers between devices with their start and end apart: 12 -> 12, of which waited for: 6 -> 8; matrix products, arithmetic and copies ran while one was open for 17% -> 22% of each run, Pallas kernels for 0% -> 0%
where the time goes in v1:
time: 843 us; the launch traced here: 842 us
  waiting for transfers between devices  604 us (72%)
  matrix products  120 us (14%)
  local copies, waits for them, and re-layouts  74.1 us (9%)
  starting transfers between devices  21.6 us (3%)
  between operations  14.2 us (2%)
    all_to_all x1, waiting for transfers between devices, local(): lax.all_to_all(jnp.stack(jnp.split(split_units(dz), lax.axis_size('tensor...  153 us
    all_to_all x1, waiting for transfers between devices, local(): lax.all_to_all(split_units(first_out), 'tensor', split_axis=1, concat_axi...  148 us
    all_to_all x1, waiting for transfers between devices, local(): lax.all_to_all(split_units(down_part), 'tensor', split_axis=1, concat_axi...  122 us
    all_to_all x1, waiting for transfers between devices, local(): lax.all_to_all(split_units(dw), 'tensor', split_axis=1, concat_axis=0, ti...  90 us
    all_gather x1, waiting for transfers between devices, fetch_second(): return lax.all_gather(shard, 'fsdp', axis=1, tiled=True)  26.1 us
    reshape x3, local copies, waits for them, and re-layouts, split_units(): return arr.reshape(arr.shape[0], NB, HB // NB, arr.shape[2])  24.2 us
    all_gather x1, waiting for transfers between devices, fetch_third(): return lax.all_gather(shard, 'fsdp', axis=1, tiled=True)  22.2 us
    all_gather x1, waiting for transfers between devices, fetch_first(): return lax.all_gather(shard, 'fsdp', axis=1, tiled=True)  21.1 us
  transfers between devices with their start and end apart: 12, of which 8 were waited for; matrix products, arithmetic and copies ran while one was open for 22% of the time, Pallas kernels for 0%

profile of v1, /device:TPU:0, one launch (start us, length us, event | category | flops | bytes accessed | tf_op | source)
XLA Modules:
  0.0 842.2 jit_solution(3518289315139058190)
XLA Ops:
  7.2 0.0 all-gather.5.cloned.1.call-start
  7.2 0.7 all-gather.5.cloned.1.call-update
  7.9 21.1 %all-gather.5.cloned.1.call-done = bf16[8,128,512]{2,1,0:T(8,128)(2,1)} async-done(((bf16[8,32,512]{2,1,0:T(8,128)(2,1)}), bf16[8,128,512]{2,1,0:T(8,128)(2,1)}) %all-gather.5.cloned.1.call-update) | async-done | bytes 1048592 | tf_op jit(solution)/shard_map/all_gather | solution.py:23
  29.0 7.5 convert_bitcast_fusion.3
  36.6 8.1 copy.55
  44.7 5.6 all-to-all-start
  50.3 0.0 all-gather.11.cloned.1.call-start
  50.4 0.9 copy.62
  51.2 0.0 all-gather.11.cloned.1.call-update
  51.2 19.4 %all-gather.11.cloned.1.call-done = bf16[8,512,128]{1,2,0:T(8,128)(2,1)} async-done(((bf16[8,128,128]{1,2,0:T(8,128)(2,1)}), bf16[8,512,128]{1,2,0:T(8,128)(2,1)}) %all-gather.11.cloned.1.call-update) | async-done | bytes 1048592 | tf_op jit(solution)/shard_map/all_gather | solution.py:35
  70.6 6.8 convert_bitcast_fusion.1
  77.5 8.1 copy.65
  85.5 148.3 %all-to-all-done = bf16[8,64,8,1024]{3,2,0,1:T(8,128)(2,1)} async-done(((bf16[8,64,8,1024]{3,2,0,1:T(8,128)(2,1)}), bf16[8,64,8,1024]{3,2,0,1:T(8,128)(2,1)}, u32[]{:S(2)}, u32[]{:S(2)}) %all-to-all-start) | async-done | bytes 8388640 | tf_op jit(solution)/shard_map/all_to_all | solution.py:63
  233.9 4.9 all-to-all-start.2
  238.8 0.0 all-gather.7.cloned.1.call-start
  238.9 0.7 all-gather.7.cloned.1.call-update
  239.6 0.2 all-gather.9.cloned.1.call-start
  239.8 1.3 copy.58
  241.1 0.0 all-gather.9.cloned.1.call-update
  241.1 8.8 %copy.56 = bf16[8,8,8,8,1024]{4,3,0,1,2:T(8,128)(2,1)} copy(bf16[8,8,8,8,1024]{4,3,0,2,1:T(8,128)(2,1)} %bitcast.1) | data formatting | bytes 16777216 | tf_op jit(solution)/shard_map/all_to_all | solution.py:63
  250.0 26.1 %all-gather.7.cloned.1.call-done = bf16[8,512,512]{2,1,0:T(8,128)(2,1)} async-done(((bf16[8,128,512]{2,1,0:T(8,128)(2,1)}), bf16[8,512,512]{2,1,0:T(8,128)(2,1)}) %all-gather.7.cloned.1.call-update) | async-done | bytes 4194320 | tf_op jit(solution)/shard_map/all_gather | solution.py:27
  276.1 14.8 %fusion.7 = (bf16[8,512,1024]{1,2,0:T(8,128)(2,1)}, f32[8,1024,512]{2,1,0:T(8,128)}) fusion(bf16[8,512,1024]{2,1,0:T(8,128)(2,1)} %bitcast.159, bf16[8,512,512]{2,1,0:T(8,128)(2,1)} %all-gather.7.cloned.1.call-done), kind=kOutput, calls=%fused_computation.10 | convolution fusion | flops 4315938816 | bytes 37748736 | tf_op jit(solution)/shard_map/cpt,cpm->cmt/dot_general | solution.py:65
  290.9 22.2 %all-gather.9.cloned.1.call-done = bf16[8,512,512]{1,2,0:T(8,128)(2,1)} async-done(((bf16[8,128,512]{1,2,0:T(8,128)(2,1)}), bf16[8,512,512]{1,2,0:T(8,128)(2,1)}) %all-gather.9.cloned.1.call-update) | async-done | bytes 4194320 | tf_op jit(solution)/shard_map/all_gather | solution.py:31
  313.2 10.2 %convert_bitcast_fusion.2 = bf16[8,64,8,1024]{3,2,1,0:T(8,128)(2,1)} fusion(bf16[8,512,1024]{1,2,0:T(8,128)(2,1)} %get-tuple-element.24, bf16[8,512,512]{1,2,0:T(8,128)(2,1)} %all-gather.9.cloned.1.call-done), kind=kOutput, calls=%fused_computation.19 | convolution fusion | flops 4299161600 | bytes 20971520 | tf_op jit(solution)/shard_map/cmt,cmn->cnt/dot_general | solution.py:67
  323.4 8.1 copy.60
  331.5 90.0 %all-to-all-done.2 = bf16[8,64,8,1024]{3,2,0,1:T(8,128)(2,1)} async-done(((bf16[8,64,8,1024]{3,2,0,1:T(8,128)(2,1)}), bf16[8,64,8,1024]{3,2,0,1:T(8,128)(2,1)}, u32[]{:S(2)}, u32[]{:S(2)}) %all-to-all-start.2) | async-done | bytes 8388640 | tf_op jit(solution)/shard_map/all_to_all | solution.py:84
  421.5 5.0 all-to-all-start.1
  426.5 0.3 reduce-scatter.9.cloned.1.call-start
  426.8 8.4 copy.66
  435.2 11.0 %convolution_convert_fusion = bf16[8,512,512]{2,1,0:T(8,128)(2,1)} fusion(bf16[8,512,1024]{1,2,0:T(8,128)(2,1)} %get-tuple-element.24, bf16[8,512,1024]{2,1,0:T(8,128)(2,1)} %bitcast.161), kind=kOutput, calls=%fused_computation.23 | convolution fusion | flops 4297064448 | bytes 20971520 | tf_op jit(solution)/shard_map/cmt,cnt->cmn/dot_general | solution.py:92
  446.2 0.0 reduce-scatter.9.cloned.1.call-update
  446.3 18.1 %fusion.5 = bf16[8,512,1024]{1,2,0:T(8,128)(2,1)} fusion(f32[8,1024,512]{2,1,0:T(8,128)} %get-tuple-element.25, bf16[8,512,1024]{2,1,0:T(8,128)(2,1)} %bitcast.162, bf16[8,512,512]{1,2,0:T(8,128)(2,1)} %all-gather.9.cloned.1.call-done), kind=kOutput, calls=%fused_computation.6 | convolution fusion | flops 4336910336 | bytes 37748736 | tf_op jit(solution)/shard_map/cnt,cmn->cmt/dot_general | solution.py:93
  464.4 12.8 %convert_bitcast_fusion = bf16[8,64,8,1024]{3,2,1,0:T(8,128)(2,1)S(1)} fusion(bf16[8,512,1024]{1,2,0:T(8,128)(2,1)} %fusion.5, bf16[8,512,512]{2,1,0:T(8,128)(2,1)S(1)} %copy-done.4), kind=kOutput, calls=%fused_computation.17 | convolution fusion | flops 4299161600 | bytes 20971520 | tf_op jit(solution)/shard_map/cmt,cpm->cpt/dot_general | solution.py:96
  477.2 1.2 fusion.48
  478.4 1.1 fusion.47
  479.4 1.1 fusion.46
  480.5 1.1 fusion.45
  481.6 1.1 fusion.44
  482.7 1.1 fusion.43
  483.8 1.1 fusion.42
  484.9 1.1 fusion.41
  486.0 122.5 %all-to-all-done.1 = bf16[8,64,8,1024]{3,2,0,1:T(8,128)(2,1)} async-done(((bf16[8,64,8,1024]{3,2,0,1:T(8,128)(2,1)}), bf16[8,64,8,1024]{3,2,0,1:T(8,128)(2,1)}, u32[]{:S(2)}, u32[]{:S(2)}) %all-to-all-start.1) | async-done | bytes 8388640 | tf_op jit(solution)/shard_map/all_to_all | solution.py:70
  608.4 5.0 all-to-all-start.3
  613.4 0.0 reduce-scatter.7.cloned.1.call-start
  613.5 12.3 %convolution_convert_fusion.1 = bf16[8,512,512]{2,1,0:T(8,128)(2,1)} fusion(bf16[8,512,1024]{2,1,0:T(8,128)(2,1)} %bitcast.160, bf16[8,512,1024]{1,2,0:T(8,128)(2,1)} %fusion.5), kind=kOutput, calls=%fused_computation.24 | convolution fusion | flops 4297064448 | bytes 20971520 | tf_op jit(solution)/shard_map/cpt,cmt->cpm/dot_general | solution.py:95
  625.8 0.0 reduce-scatter.7.cloned.1.call-update
  625.8 0.3 reduce-scatter.11.cloned.1.call-start
  626.2 9.1 %copy.61 = bf16[8,8,8,8,1024]{4,3,1,0,2:T(8,128)(2,1)} copy(bf16[8,8,8,8,1024]{4,3,1,2,0:T(8,128)(2,1)} %bitcast.10) | data formatting | bytes 16777216 | tf_op jit(solution)/shard_map/all_to_all | solution.py:70
  635.3 7.1 fusion.28
  642.4 0.0 reduce-scatter.11.cloned.1.call-update
  642.4 0.0 reduce-scatter.5.cloned.1.call-start
  642.5 153.2 %all-to-all-done.3 = bf16[8,8,8,8,1024]{4,3,2,1,0:T(8,128)(2,1)} async-done(((bf16[8,8,8,8,1024]{4,3,2,1,0:T(8,128)(2,1)}), bf16[8,8,8,8,1024]{4,3,2,1,0:T(8,128)(2,1)}, u32[]{:S(2)}, u32[]{:S(2)}) %all-to-all-start.3) | async-done | bytes 8388640 | tf_op jit(solution)/shard_map/all_to_all | solution.py:99
  795.6 7.3 fusion.36
  802.9 2.8 copy.72
  805.7 0.0 reduce-scatter.5.cloned.1.call-update
  805.7 0.0 reduce-scatter.9.cloned.1.call-done
  805.7 2.8 convert_element_type.83
  808.5 3.0 convert_element_type.81
  811.5 6.1 convolution_convert_fusion.2
  817.6 3.9 copy.76
  821.5 6.3 fusion.21
  827.8 3.9 copy.77
  831.8 1.8 convert_element_type.85
  833.6 1.8 copy.78
  (13 shorter events, 0.0 us)
Async XLA Ops:
  7.2 63.5 %copy-start = (bf16[1024,1024]{1,0:T(8,128)(2,1)S(1)}, bf16[1024,1024]{1,0:T(8,128)(2,1)}, u32[]{:S(2)}) copy-start(bf16[1024,1024]{1,0:T(8,128)(2,1)} %param.11) | copy-start | bytes 6291460
  7.2 21.9 %all-gather.5.cloned.1.call-start = ((), (), s32[]{:S(2)}) async-start(), calls=%async_computation.8 | async-start | bytes 1310720 | tf_op jit(solution)/shard_map/all_gather | solution.py:23
  44.7 5.7 copy-start.3
  44.7 189.2 %all-to-all-start = ((bf16[8,64,8,1024]{3,2,0,1:T(8,128)(2,1)}), bf16[8,64,8,1024]{3,2,0,1:T(8,128)(2,1)}, u32[]{:S(2)}, u32[]{:S(2)}) async-start(bf16[8,64,8,1024]{3,2,0,1:T(8,128)(2,1)} %copy.55), calls=%async_computation | async-start | bytes 16777216 | tf_op jit(solution)/shard_map/all_to_all | solution.py:63
  50.3 20.3 %all-gather.11.cloned.1.call-start = ((), (), s32[]{:S(2)}) async-start(), calls=%async_computation.11 | async-start | bytes 1310720 | tf_op jit(solution)/shard_map/all_gather | solution.py:35
  85.5 154.3 %copy-start.2 = (bf16[8,128,512]{2,1,0:T(8,128)(2,1)S(1)}, bf16[8,128,512]{2,1,0:T(8,128)(2,1)}, u32[]{:S(2)}) copy-start(bf16[8,128,512]{2,1,0:T(8,128)(2,1)} %param.9) | copy-start | bytes 3145732
  233.9 187.6 %all-to-all-start.2 = ((bf16[8,64,8,1024]{3,2,0,1:T(8,128)(2,1)}), bf16[8,64,8,1024]{3,2,0,1:T(8,128)(2,1)}, u32[]{:S(2)}, u32[]{:S(2)}) async-start(bf16[8,64,8,1024]{3,2,0,1:T(8,128)(2,1)} %copy.65), calls=%async_computation.2 | async-start | bytes 16777216 | tf_op jit(solution)/shard_map/all_to_all | solution.py:84
  238.8 37.3 %all-gather.7.cloned.1.call-start = ((), (), s32[]{:S(2)}) async-start(), calls=%async_computation.9 | async-start | bytes 5242880 | tf_op jit(solution)/shard_map/all_gather | solution.py:27
  239.6 73.6 %all-gather.9.cloned.1.call-start = ((), (), s32[]{:S(2)}) async-start(), calls=%async_computation.10 | async-start | bytes 5242880 | tf_op jit(solution)/shard_map/all_gather | solution.py:31
  421.5 187.0 %all-to-all-start.1 = ((bf16[8,64,8,1024]{3,2,0,1:T(8,128)(2,1)}), bf16[8,64,8,1024]{3,2,0,1:T(8,128)(2,1)}, u32[]{:S(2)}, u32[]{:S(2)}) async-start(bf16[8,64,8,1024]{3,2,0,1:T(8,128)(2,1)} %copy.60), calls=%async_computation.1 | async-start | bytes 16777216 | tf_op jit(solution)/shard_map/all_to_all | solution.py:70
  426.5 379.2 %reduce-scatter.9.cloned.1.call-start = ((), (), s32[]{:S(2)}) async-start(), calls=%async_computation.14 | async-start | bytes 5242880 | tf_op jit(solution)/shard_map/reduce_scatter | solution.py:118
  446.3 18.2 %copy-start.4 = (bf16[8,512,512]{2,1,0:T(8,128)(2,1)S(1)}, bf16[8,512,512]{2,1,0:T(8,128)(2,1)}, u32[]{:S(2)}) copy-start(bf16[8,512,512]{2,1,0:T(8,128)(2,1)} %all-gather.7.cloned.1.call-done) | copy-start | bytes 12582916
  608.4 187.2 %all-to-all-start.3 = ((bf16[8,8,8,8,1024]{4,3,2,1,0:T(8,128)(2,1)}), bf16[8,8,8,8,1024]{4,3,2,1,0:T(8,128)(2,1)}, u32[]{:S(2)}, u32[]{:S(2)}) async-start(bf16[8,8,8,8,1024]{4,3,2,1,0:T(8,128)(2,1)} %fusion.41), calls=%async_computation.3 | async-start | bytes 16777216 | tf_op jit(solution)/shard_map/all_to_all | solution.py:99
  613.4 195.1 %reduce-scatter.7.cloned.1.call-start = ((), (), s32[]{:S(2)}) async-start(), calls=%async_computation.13 | async-start | bytes 5242880 | tf_op jit(solution)/shard_map/reduce_scatter | solution.py:115
  625.8 205.9 %reduce-scatter.11.cloned.1.call-start = ((), (), s32[]{:S(2)}) async-start(), calls=%async_computation.15 | async-start | bytes 1310720 | tf_op jit(solution)/shard_map/reduce_scatter | solution.py:121
  642.4 191.2 %reduce-scatter.5.cloned.1.call-start = ((), (), s32[]{:S(2)}) async-start(), calls=%async_computation.12 | async-start | bytes 1310720 | tf_op jit(solution)/shard_map/reduce_scatter | solution.py:112
  802.9 8.6 %copy-start.1 = (bf16[8,512,128]{1,2,0:T(8,128)(2,1)S(1)}, bf16[8,512,128]{1,2,0:T(8,128)(2,1)}, u32[]{:S(2)}) copy-start(bf16[8,512,128]{1,2,0:T(8,128)(2,1)} %all-gather.11.cloned.1.call-done) | copy-start | bytes 3145732
Sparse Core Ops, SparseCore 0:
  9.6 19.4 all-gather.4
  53.3 17.3 all-gather.10
  241.2 34.8 all-gather.6
  278.1 35.0 all-gather.8
  446.4 44.6 reduce-scatter.8
  626.0 44.8 reduce-scatter.6
  673.3 24.8 reduce-scatter.10
  805.8 23.2 reduce-scatter.4
